TPU v7x, 128 devices: a whole 4x4x4 slice. The times are simulated.
128 devices in a mesh: dom: 16 (over y_lo, z, core), rep: 8 (over y_hi, x).
Axes of the slice: x: 4, y: 4 (y_hi: 2, y_lo: 2; y = y_hi * 2 + y_lo), z: 4, core: 2. Of those that a mesh axis runs over, the one named last changes fastest.
Arguments:
- node_features: bfloat16 [65536, 256], P(('dom', 'rep')), may hold values from -6 to 6
- weight: bfloat16 [256, 256], replicated, may hold values from -0.375 to 0.375
- cotangent: bfloat16 [65536, 256], P(('dom', 'rep')), may hold values from -6 to 6
- tile_row: int32 [16, 8, 512], P('dom', 'rep'), may hold values from 0 to 31
- tile_col: int32 [16, 8, 512], P('dom', 'rep'), may hold values from 0 to 63
- tile_values: bfloat16 [16, 8, 512, 128, 128], P('dom', 'rep'), may hold values from -0.0625 to 0.0625
- tile_count: int32 [16, 8], P('dom', 'rep'), may hold values from 128 to 512, as said below
Outputs:
- output: bfloat16 [65536, 256], P(('dom', 'rep'))
- grad_features: bfloat16 [65536, 256], P(('dom', 'rep'))
- grad_weight: float32 [256, 256], replicated
Inputs may be any that keep to these rules, and one draw needn't show every extreme that they name: Live slots are the first tile_count slots of each device's list; some device has all 512 slots live.
All inputs are finite; a program needn't handle non-finite values.
Results may differ from a plain program's by a relative error of at most 0.0061.
Values may be sent and summed in bfloat16 or wider, within the bound.
No kernel may reach another device: no remote copies, remote signals or barrier semaphores. Data moves between devices by JAX's collectives and lax.ppermute only.
A program may use at most 192 MiB of HBM per device.

v0:
```python
import jax
import jax.numpy as jnp
from jax import lax
from jax.sharding import PartitionSpec as P


def silu_slope(summed):
    sig = jax.nn.sigmoid(summed)
    return sig * (1.0 + summed * (1.0 - sig))


def tile_products(values, pick_index, place_index, active, source, out_blocks, flipped):
    slots = values.shape[0]
    feature_width = source.shape[2]
    per_turn = min(slots, 128)
    pattern = "tba,tbf->taf" if flipped else "tab,tbf->taf"

    def accumulate(turn_index, summed):
        first_slot = turn_index * per_turn
        block_values = lax.dynamic_slice_in_dim(values, first_slot, per_turn, 0)
        picks = lax.dynamic_slice_in_dim(pick_index, first_slot, per_turn, 0)
        picked = jnp.take(source, picks, axis=0)
        products = jnp.einsum(pattern, block_values, picked, preferred_element_type=jnp.float32)
        places = lax.dynamic_slice_in_dim(place_index, first_slot, per_turn, 0)
        enabled = lax.dynamic_slice_in_dim(active, first_slot, per_turn, 0)
        products = products * enabled.astype(jnp.float32)[:, None, None]
        return summed.at[places].add(products)

    initial = jnp.zeros((out_blocks, 128, feature_width), jnp.float32)
    summed = lax.fori_loop(0, slots // per_turn, accumulate, initial)
    return summed.reshape(out_blocks * 128, feature_width)


def body(node_features, weight, cotangent, tile_row, tile_col, tile_values, tile_count):
    rows_here = node_features.shape[0]
    feature_width = weight.shape[0]
    dom_size = lax.axis_size("dom")
    rep_size = lax.axis_size("rep")
    slots = tile_row.shape[2]
    row_index = tile_row.reshape(slots)
    col_index = tile_col.reshape(slots)
    values = tile_values.reshape(slots, 128, 128)
    active = lax.broadcasted_iota(jnp.int32, (slots,), 0) < tile_count.reshape(())
    projected = jnp.dot(node_features, weight, preferred_element_type=jnp.float32).astype(
        jnp.bfloat16
    )
    gathered = lax.all_gather(projected, "dom", axis=0, tiled=True)
    source = gathered.reshape(-1, 128, feature_width)
    part_blocks = rep_size * rows_here // 128
    partial_value = tile_products(values, col_index, row_index, active, source, part_blocks, False)
    summed = lax.psum_scatter(partial_value, "rep", scatter_dimension=0, tiled=True)
    output = jax.nn.silu(summed).astype(jnp.bfloat16)
    grad_own = (cotangent.astype(jnp.float32) * silu_slope(summed)).astype(jnp.bfloat16)
    grad_block = lax.all_gather(grad_own, "rep", axis=0, tiled=True)
    back_blocks = dom_size * rows_here // 128
    back_partial = tile_products(
        values,
        row_index,
        col_index,
        active,
        grad_block.reshape(-1, 128, feature_width),
        back_blocks,
        True,
    )
    grad_projected = lax.psum_scatter(back_partial, "dom", scatter_dimension=0, tiled=True).astype(
        jnp.bfloat16
    )
    grad_features = jnp.dot(grad_projected, weight.T, preferred_element_type=jnp.float32).astype(
        jnp.bfloat16
    )
    local_weight = jnp.dot(node_features.T, grad_projected, preferred_element_type=jnp.float32)
    grad_weight = lax.psum(local_weight, ("dom", "rep"))
    return (output, grad_features, grad_weight)


def solution(mesh):
    placed = (
        P(("dom", "rep"), None),
        P(),
        P(("dom", "rep"), None),
        P("dom", "rep", None),
        P("dom", "rep", None),
        P("dom", "rep", None, None, None),
        P("dom", "rep"),
    )
    return jax.shard_map(
        body,
        mesh=mesh,
        in_specs=placed,
        out_specs=(P(("dom", "rep"), None), P(("dom", "rep"), None), P()),
        check_vma=False,
    )
```

profile of v0, /device:TPU:1, one launch (start us, length us, event | category | flops | bytes accessed | tf_op | source)
XLA Modules:
  0.0 908.0 jit_solution(10777865380881318707)
XLA Ops:
  7.2 0.0 all-gather.3.cloned.1.call-start
  7.2 0.9 copy-done
  8.1 1.8 convolution_convert_fusion.1
  10.0 0.0 reduce-scatter.3.cloned.1.call-start
  10.7 40.7 %all-gather.3.cloned.1.call-done = bf16[8192,256]{1,0:T(8,128)(2,1)} async-done(((bf16[512,256]{1,0:T(8,128)(2,1)}), bf16[8192,256]{1,0:T(8,128)(2,1)}) %all-gather.3.cloned.1.call-update) | async-done | bytes 4194320 | tf_op jit(solution)/shard_map/all_gather | solution.py:47
  51.4 2.4 broadcast_in_dim.74
  53.8 244.2 %while.26 = (s32[]{:T(128)}, f32[32,128,256]{2,1,0:T(8,128)}, s32[512]{0:T(512)}, bf16[512,128,128]{2,1,0:T(8,128)(2,1)}, s32[512]{0:T(512)}, /*index=5*/bf16[64...) while((s32[]{:T(128)}, f32[32,128,256]{2,1,0:T(8,128)}, ...), condition=%wide.region_2.3_spmd, body=%wide.region_0.2_spmd.sunk | while | flops 1086327040 | bytes 96478248 | solution.py:30
  53.8 0.8 compare_and_fusion.4
  54.6 8.8 gather_fusion
  63.4 12.8 %convolution_multiply_fusion.4 = f32[128,128,256]{2,1,0:T(8,128)} fusion(f32[128]{0:T(128)S(1)} %get-tuple-element.384, bf16[128,128,256]{2,1,0:T(8,128)(2,1)} %gather_fusion, pred[128]{0:T(512)(128)(4,1)S(1)} %get-tuple-element.386, bf16[512,128,128]{2,1,0:T(8,128)(2,1)} %get-tuple-element.422, s32[]{:T(128)S(6)} %select_n.85), kind=kOutput, calls=%fused_computation.4.clone.1 | convolution fusion | flops 1082130432 | bytes 29360772 | tf_op jit(solution)/shard_map/while/body/eval_jaxpr/tab,tbf->taf/dot_general | solution.py:23
  76.2 0.8 compare_select_fusion.8
  76.9 38.1 %scatter_fusion = f32[32,128,256]{2,1,0:T(8,128)} fusion(f32[32,128,256]{2,1,0:T(8,128)} %get-tuple-element.409, s32[128]{0:T(128)S(1)} %compare_select_fusion.8, f32[128,128,256]{2,1,0:T(8,128)} %convolution_multiply_fusion.4), kind=kCustom, calls=%fused_computation.2.clone.1 | custom fusion | flops 4194304 | bytes 50332160 | tf_op jit(solution)/shard_map/while/body/eval_jaxpr/scatter-add | solution.py:27
  115.0 0.8 compare_and_fusion.4
  115.8 8.8 gather_fusion
  124.5 12.8 %convolution_multiply_fusion.4 = f32[128,128,256]{2,1,0:T(8,128)} fusion(f32[128]{0:T(128)S(1)} %get-tuple-element.384, bf16[128,128,256]{2,1,0:T(8,128)(2,1)} %gather_fusion, pred[128]{0:T(512)(128)(4,1)S(1)} %get-tuple-element.386, bf16[512,128,128]{2,1,0:T(8,128)(2,1)} %get-tuple-element.422, s32[]{:T(128)S(6)} %select_n.85), kind=kOutput, calls=%fused_computation.4.clone.1 | convolution fusion | flops 1082130432 | bytes 29360772 | tf_op jit(solution)/shard_map/while/body/eval_jaxpr/tab,tbf->taf/dot_general | solution.py:23
  137.3 0.8 compare_select_fusion.8
  138.1 38.1 %scatter_fusion = f32[32,128,256]{2,1,0:T(8,128)} fusion(f32[32,128,256]{2,1,0:T(8,128)} %get-tuple-element.409, s32[128]{0:T(128)S(1)} %compare_select_fusion.8, f32[128,128,256]{2,1,0:T(8,128)} %convolution_multiply_fusion.4), kind=kCustom, calls=%fused_computation.2.clone.1 | custom fusion | flops 4194304 | bytes 50332160 | tf_op jit(solution)/shard_map/while/body/eval_jaxpr/scatter-add | solution.py:27
  176.2 0.8 compare_and_fusion.4
  176.9 8.8 gather_fusion
  185.7 12.8 %convolution_multiply_fusion.4 = f32[128,128,256]{2,1,0:T(8,128)} fusion(f32[128]{0:T(128)S(1)} %get-tuple-element.384, bf16[128,128,256]{2,1,0:T(8,128)(2,1)} %gather_fusion, pred[128]{0:T(512)(128)(4,1)S(1)} %get-tuple-element.386, bf16[512,128,128]{2,1,0:T(8,128)(2,1)} %get-tuple-element.422, s32[]{:T(128)S(6)} %select_n.85), kind=kOutput, calls=%fused_computation.4.clone.1 | convolution fusion | flops 1082130432 | bytes 29360772 | tf_op jit(solution)/shard_map/while/body/eval_jaxpr/tab,tbf->taf/dot_general | solution.py:23
  198.5 0.8 compare_select_fusion.8
  199.3 37.7 %scatter_fusion = f32[32,128,256]{2,1,0:T(8,128)} fusion(f32[32,128,256]{2,1,0:T(8,128)} %get-tuple-element.409, s32[128]{0:T(128)S(1)} %compare_select_fusion.8, f32[128,128,256]{2,1,0:T(8,128)} %convolution_multiply_fusion.4), kind=kCustom, calls=%fused_computation.2.clone.1 | custom fusion | flops 4194304 | bytes 50332160 | tf_op jit(solution)/shard_map/while/body/eval_jaxpr/scatter-add | solution.py:27
  237.0 0.8 compare_and_fusion.4
  237.7 8.8 gather_fusion
  246.5 12.8 %convolution_multiply_fusion.4 = f32[128,128,256]{2,1,0:T(8,128)} fusion(f32[128]{0:T(128)S(1)} %get-tuple-element.384, bf16[128,128,256]{2,1,0:T(8,128)(2,1)} %gather_fusion, pred[128]{0:T(512)(128)(4,1)S(1)} %get-tuple-element.386, bf16[512,128,128]{2,1,0:T(8,128)(2,1)} %get-tuple-element.422, s32[]{:T(128)S(6)} %select_n.85), kind=kOutput, calls=%fused_computation.4.clone.1 | convolution fusion | flops 1082130432 | bytes 29360772 | tf_op jit(solution)/shard_map/while/body/eval_jaxpr/tab,tbf->taf/dot_general | solution.py:23
  259.3 0.8 compare_select_fusion.8
  260.1 37.9 %scatter_fusion = f32[32,128,256]{2,1,0:T(8,128)} fusion(f32[32,128,256]{2,1,0:T(8,128)} %get-tuple-element.409, s32[128]{0:T(128)S(1)} %compare_select_fusion.8, f32[128,128,256]{2,1,0:T(8,128)} %convolution_multiply_fusion.4), kind=kCustom, calls=%fused_computation.2.clone.1 | custom fusion | flops 4194304 | bytes 50332160 | tf_op jit(solution)/shard_map/while/body/eval_jaxpr/scatter-add | solution.py:27
  298.0 0.0 reduce-scatter.3.cloned.1.call-update
  298.0 0.0 all-gather.5.cloned.1.call-start
  298.0 83.2 %reduce-scatter.3.cloned.1.call-done = f32[512,256]{1,0:T(8,128)} async-done(((f32[4096,256]{1,0:T(8,128)}), f32[512,256]{1,0:T(8,128)}) %reduce-scatter.3.cloned.1.call-update) | async-done | bytes 524304 | tf_op jit(solution)/shard_map/reduce_scatter | solution.py:51
  381.3 2.1 multiply_convert_fusion
  383.4 0.0 all-gather.5.cloned.1.call-update
  383.4 0.2 reduce-scatter.5.cloned.1.call-start
  383.6 22.4 %copy.10 = bf16[1,1,512,128,128]{3,4,2,1,0:T(8,128)(2,1)} copy(bf16[1,1,512,128,128]{4,3,2,1,0:T(8,128)(2,1)} %bitcast.21) | data formatting | bytes 33554432 | tf_op args[5]
  406.0 31.9 %all-gather.5.cloned.1.call-done = bf16[4096,256]{1,0:T(8,128)(2,1)} async-done(((bf16[512,256]{1,0:T(8,128)(2,1)}), bf16[4096,256]{1,0:T(8,128)(2,1)}) %all-gather.5.cloned.1.call-update) | async-done | bytes 2097168 | tf_op jit(solution)/shard_map/all_gather | solution.py:54
  437.9 4.2 broadcast_in_dim.75
  442.1 236.8 %while.27 = (s32[]{:T(128)}, f32[64,128,256]{2,1,0:T(8,128)}, s32[512]{0:T(512)}, bf16[512,128,128]{1,2,0:T(8,128)(2,1)}, s32[512]{0:T(512)}, /*index=5*/bf16[32...) while((s32[]{:T(128)}, f32[64,128,256]{2,1,0:T(8,128)}, ...), condition=%wide.region_6.7_spmd, body=%wide.region_4.6_spmd.sunk | while | flops 1086327040 | bytes 96478248 | solution.py:30
  442.1 0.8 compare_and_fusion.5
  442.9 6.6 gather_fusion.1
  449.5 12.8 %convolution_multiply_fusion.5 = f32[128,128,256]{2,1,0:T(8,128)} fusion(f32[128]{0:T(128)S(1)} %get-tuple-element.394, bf16[128,128,256]{2,1,0:T(8,128)(2,1)} %gather_fusion.1, pred[128]{0:T(512)(128)(4,1)S(1)} %get-tuple-element.396, bf16[512,128,128]{1,2,0:T(8,128)(2,1)} %get-tuple-element.455, s32[]{:T(128)S(6)} %select_n.88), kind=kOutput, calls=%fused_computation.16.clone.1 | convolution fusion | flops 1082130432 | bytes 29360772 | tf_op jit(solution)/shard_map/while/body/eval_jaxpr/tba,tbf->taf/dot_general | solution.py:23
  462.3 0.8 compare_select_fusion.9
  463.1 38.5 %scatter_fusion.1 = f32[64,128,256]{2,1,0:T(8,128)} fusion(f32[64,128,256]{2,1,0:T(8,128)} %get-tuple-element.442, s32[128]{0:T(128)S(1)} %compare_select_fusion.9, f32[128,128,256]{2,1,0:T(8,128)} %convolution_multiply_fusion.5), kind=kCustom, calls=%fused_computation.3.clone.1 | custom fusion | flops 4194304 | bytes 50332160 | tf_op jit(solution)/shard_map/while/body/eval_jaxpr/scatter-add | solution.py:27
  501.6 0.8 compare_and_fusion.5
  502.3 6.6 gather_fusion.1
  508.9 12.8 %convolution_multiply_fusion.5 = f32[128,128,256]{2,1,0:T(8,128)} fusion(f32[128]{0:T(128)S(1)} %get-tuple-element.394, bf16[128,128,256]{2,1,0:T(8,128)(2,1)} %gather_fusion.1, pred[128]{0:T(512)(128)(4,1)S(1)} %get-tuple-element.396, bf16[512,128,128]{1,2,0:T(8,128)(2,1)} %get-tuple-element.455, s32[]{:T(128)S(6)} %select_n.88), kind=kOutput, calls=%fused_computation.16.clone.1 | convolution fusion | flops 1082130432 | bytes 29360772 | tf_op jit(solution)/shard_map/while/body/eval_jaxpr/tba,tbf->taf/dot_general | solution.py:23
  521.7 0.8 compare_select_fusion.9
  522.5 38.1 %scatter_fusion.1 = f32[64,128,256]{2,1,0:T(8,128)} fusion(f32[64,128,256]{2,1,0:T(8,128)} %get-tuple-element.442, s32[128]{0:T(128)S(1)} %compare_select_fusion.9, f32[128,128,256]{2,1,0:T(8,128)} %convolution_multiply_fusion.5), kind=kCustom, calls=%fused_computation.3.clone.1 | custom fusion | flops 4194304 | bytes 50332160 | tf_op jit(solution)/shard_map/while/body/eval_jaxpr/scatter-add | solution.py:27
  560.6 0.8 compare_and_fusion.5
  561.3 6.6 gather_fusion.1
  567.9 12.8 %convolution_multiply_fusion.5 = f32[128,128,256]{2,1,0:T(8,128)} fusion(f32[128]{0:T(128)S(1)} %get-tuple-element.394, bf16[128,128,256]{2,1,0:T(8,128)(2,1)} %gather_fusion.1, pred[128]{0:T(512)(128)(4,1)S(1)} %get-tuple-element.396, bf16[512,128,128]{1,2,0:T(8,128)(2,1)} %get-tuple-element.455, s32[]{:T(128)S(6)} %select_n.88), kind=kOutput, calls=%fused_computation.16.clone.1 | convolution fusion | flops 1082130432 | bytes 29360772 | tf_op jit(solution)/shard_map/while/body/eval_jaxpr/tba,tbf->taf/dot_general | solution.py:23
  580.7 0.8 compare_select_fusion.9
  581.5 38.3 %scatter_fusion.1 = f32[64,128,256]{2,1,0:T(8,128)} fusion(f32[64,128,256]{2,1,0:T(8,128)} %get-tuple-element.442, s32[128]{0:T(128)S(1)} %compare_select_fusion.9, f32[128,128,256]{2,1,0:T(8,128)} %convolution_multiply_fusion.5), kind=kCustom, calls=%fused_computation.3.clone.1 | custom fusion | flops 4194304 | bytes 50332160 | tf_op jit(solution)/shard_map/while/body/eval_jaxpr/scatter-add | solution.py:27
  619.8 0.8 compare_and_fusion.5
  620.5 6.6 gather_fusion.1
  627.1 12.8 %convolution_multiply_fusion.5 = f32[128,128,256]{2,1,0:T(8,128)} fusion(f32[128]{0:T(128)S(1)} %get-tuple-element.394, bf16[128,128,256]{2,1,0:T(8,128)(2,1)} %gather_fusion.1, pred[128]{0:T(512)(128)(4,1)S(1)} %get-tuple-element.396, bf16[512,128,128]{1,2,0:T(8,128)(2,1)} %get-tuple-element.455, s32[]{:T(128)S(6)} %select_n.88), kind=kOutput, calls=%fused_computation.16.clone.1 | convolution fusion | flops 1082130432 | bytes 29360772 | tf_op jit(solution)/shard_map/while/body/eval_jaxpr/tba,tbf->taf/dot_general | solution.py:23
  639.9 0.8 compare_select_fusion.9
  640.7 38.3 %scatter_fusion.1 = f32[64,128,256]{2,1,0:T(8,128)} fusion(f32[64,128,256]{2,1,0:T(8,128)} %get-tuple-element.442, s32[128]{0:T(128)S(1)} %compare_select_fusion.9, f32[128,128,256]{2,1,0:T(8,128)} %convolution_multiply_fusion.5), kind=kCustom, calls=%fused_computation.3.clone.1 | custom fusion | flops 4194304 | bytes 50332160 | tf_op jit(solution)/shard_map/while/body/eval_jaxpr/scatter-add | solution.py:27
  679.0 0.0 reduce-scatter.5.cloned.1.call-update
  679.0 0.0 all-reduce.2.cloned.1.call-start
  679.0 71.8 %reduce-scatter.5.cloned.1.call-done = f32[512,256]{1,0:T(8,128)} async-done(((f32[8192,256]{1,0:T(8,128)}), f32[512,256]{1,0:T(8,128)}) %reduce-scatter.5.cloned.1.call-update) | async-done | bytes 524304 | tf_op jit(solution)/shard_map/reduce_scatter | solution.py:65
  750.8 2.0 convolution_bitcast_fusion
  752.9 2.0 convolution_convert_fusion
  754.9 144.8 %all-reduce.2.cloned.1.call-done = f32[256,256]{0,1:T(8,128)} async-done(((f32[256,256]{0,1:T(8,128)}), f32[256,256]{0,1:T(8,128)}) %all-reduce.2.cloned.1.call-update) | async-done | bytes 262160 | tf_op jit(solution)/shard_map/psum | solution.py:72
  899.6 1.8 copy.12
  (18 shorter events, 0.1 us)
Async XLA Ops:
  7.2 1.0 copy-start
  7.2 44.2 %all-gather.3.cloned.1.call-start = ((), (), s32[]{:S(2)}) async-start(), calls=%async_computation.2 | async-start | bytes 4456448 | tf_op jit(solution)/shard_map/all_gather | solution.py:47
  10.0 371.3 %reduce-scatter.3.cloned.1.call-start = ((), (), s32[]{:S(2)}) async-start(), calls=%async_computation.3 | async-start | bytes 4718592 | tf_op jit(solution)/shard_map/reduce_scatter | solution.py:51
  53.8 327.5 %copy-start.3 = (bf16[512,256]{1,0:T(8,128)(2,1)S(1)}, bf16[512,256]{1,0:T(8,128)(2,1)}, u32[]{:S(2)}) copy-start(bf16[512,256]{1,0:T(8,128)(2,1)} %param.13) | copy-start | bytes 786436
  298.0 139.9 %all-gather.5.cloned.1.call-start = ((), (), s32[]{:S(2)}) async-start(), calls=%async_computation.4 | async-start | bytes 2359296 | tf_op jit(solution)/shard_map/all_gather | solution.py:54
  383.4 367.4 %reduce-scatter.5.cloned.1.call-start = ((), (), s32[]{:S(2)}) async-start(), calls=%async_computation.5 | async-start | bytes 8912896 | tf_op jit(solution)/shard_map/reduce_scatter | solution.py:65
  437.9 4.2 copy-start.1
  679.0 73.9 %copy-start.2 = (bf16[256,256]{1,0:T(8,128)(2,1)S(1)}, bf16[256,256]{1,0:T(8,128)(2,1)}, u32[]{:S(2)}) copy-start(bf16[256,256]{1,0:T(8,128)(2,1)} %param.12) | copy-start | bytes 393220
  679.0 220.6 %all-reduce.2.cloned.1.call-start = ((), (), s32[]{:S(2)}) async-start(), calls=%async_computation.6 | async-start | bytes 524288 | tf_op jit(solution)/shard_map/psum | solution.py:72
Sparse Core Ops, SparseCore 0:
  10.3 41.0 all-gather.2
  298.1 83.1 reduce-scatter.2
  384.2 53.6 all-gather.4
  679.1 71.6 reduce-scatter.4
  756.0 143.6 all-reduce.1
where the time goes:
time: 910 us; the launch traced here: 908 us
  waiting for transfers between devices  372 us (41%)
  other arithmetic  319 us (35%)
  matrix products  108 us (12%)
  local copies, waits for them, and re-layouts  93.1 us (10%)
  between operations  14.5 us (2%)
    scatter-add x8, other arithmetic, accumulate(): return summed.at[places].add(products)  305 us
    psum x1, waiting for transfers between devices, body(): grad_weight = lax.psum(local_weight, ('dom', 'rep'))  145 us
    dot_general x8, matrix products, accumulate(): jnp.einsum(pattern, block_values, picked, preferred_element_type=jnp.floa...  103 us
    reduce_scatter x1, waiting for transfers between devices, body(): lax.psum_scatter(partial_value, 'rep', scatter_dimension=0, tiled=True)  83.2 us
    reduce_scatter x1, waiting for transfers between devices, body(): lax.psum_scatter(back_partial, 'dom', scatter_dimension=0, tiled=True)  71.8 us
    gather x8, local copies, waits for them, and re-layouts, accumulate(): picked = jnp.take(source, picks, axis=0)  61.3 us
    all_gather x1, waiting for transfers between devices, body(): gathered = lax.all_gather(projected, 'dom', axis=0, tiled=True)  40.7 us
    all_gather x1, waiting for transfers between devices, body(): grad_block = lax.all_gather(grad_own, 'rep', axis=0, tiled=True)  31.9 us
  transfers between devices with their start and end apart: 5, of which 5 were waited for; matrix products, arithmetic and copies ran while one was open for 3% of the time, Pallas kernels for 0%

commit v1 on v0

--- a/solution.py
+++ b/solution.py
@@ -69,7 +69,7 @@
         jnp.bfloat16
     )
     local_weight = jnp.dot(node_features.T, grad_projected, preferred_element_type=jnp.float32)
-    grad_weight = lax.psum(local_weight, ("dom", "rep"))
+    grad_weight = lax.psum(lax.psum(local_weight, "dom"), "rep")
     return (output, grad_features, grad_weight)
 
 

time: 910 us -> 970 us (1.066)
  waiting for transfers between devices: 372 us -> 428 us
    psum x1 -> x2, waiting for transfers between devices: 145 us -> 200 us  [body(): grad_weight = lax.psum(lax.psum(local_weight, 'dom'), 'rep')]
  transfers between devices with their start and end apart: 5 -> 6, of which waited for: 5 -> 6; matrix products, arithmetic and copies ran while one was open for 3% -> 3% of each run, Pallas kernels for 0% -> 0%
where the time goes in v1:
time: 970 us; the launch traced here: 964 us
  waiting for transfers between devices  428 us (44%)
  other arithmetic  319 us (33%)
  matrix products  108 us (11%)
  local copies, waits for them, and re-layouts  93.1 us (10%)
  between operations  14.8 us (2%)
    scatter-add x8, other arithmetic, accumulate(): return summed.at[places].add(products)  305 us
    psum x2, waiting for transfers between devices, body(): grad_weight = lax.psum(lax.psum(local_weight, 'dom'), 'rep')  200 us
    dot_general x8, matrix products, accumulate(): jnp.einsum(pattern, block_values, picked, preferred_element_type=jnp.floa...  103 us
    reduce_scatter x1, waiting for transfers between devices, body(): lax.psum_scatter(partial_value, 'rep', scatter_dimension=0, tiled=True)  83.2 us
    reduce_scatter x1, waiting for transfers between devices, body(): lax.psum_scatter(back_partial, 'dom', scatter_dimension=0, tiled=True)  71.8 us
    gather x8, local copies, waits for them, and re-layouts, accumulate(): picked = jnp.take(source, picks, axis=0)  61.3 us
    all_gather x1, waiting for transfers between devices, body(): gathered = lax.all_gather(projected, 'dom', axis=0, tiled=True)  40.7 us
    all_gather x1, waiting for transfers between devices, body(): grad_block = lax.all_gather(grad_own, 'rep', axis=0, tiled=True)  31.9 us
  transfers between devices with their start and end apart: 6, of which 6 were waited for; matrix products, arithmetic and copies ran while one was open for 3% of the time, Pallas kernels for 0%

profile of v1, /device:TPU:1, one launch (start us, length us, event | category | flops | bytes accessed | tf_op | source)
XLA Modules:
  0.0 963.6 jit_solution(4161068462464806824)
XLA Ops:
  7.2 0.0 all-gather.3.cloned.1.call-start
  7.2 0.9 copy-done
  8.1 1.8 convolution_convert_fusion.1
  10.0 0.0 reduce-scatter.3.cloned.1.call-start
  10.7 40.7 %all-gather.3.cloned.1.call-done = bf16[8192,256]{1,0:T(8,128)(2,1)} async-done(((bf16[512,256]{1,0:T(8,128)(2,1)}), bf16[8192,256]{1,0:T(8,128)(2,1)}) %all-gather.3.cloned.1.call-update) | async-done | bytes 4194320 | tf_op jit(solution)/shard_map/all_gather | solution.py:47
  51.4 2.4 broadcast_in_dim.74
  53.8 244.2 %while.26 = (s32[]{:T(128)}, f32[32,128,256]{2,1,0:T(8,128)}, s32[512]{0:T(512)}, bf16[512,128,128]{2,1,0:T(8,128)(2,1)}, s32[512]{0:T(512)}, /*index=5*/bf16[64...) while((s32[]{:T(128)}, f32[32,128,256]{2,1,0:T(8,128)}, ...), condition=%wide.region_2.3_spmd, body=%wide.region_0.2_spmd.sunk | while | flops 1086327040 | bytes 96478248 | solution.py:30
  53.8 0.8 compare_and_fusion.4
  54.6 8.8 gather_fusion
  63.4 12.8 %convolution_multiply_fusion.4 = f32[128,128,256]{2,1,0:T(8,128)} fusion(f32[128]{0:T(128)S(1)} %get-tuple-element.384, bf16[128,128,256]{2,1,0:T(8,128)(2,1)} %gather_fusion, pred[128]{0:T(512)(128)(4,1)S(1)} %get-tuple-element.386, bf16[512,128,128]{2,1,0:T(8,128)(2,1)} %get-tuple-element.422, s32[]{:T(128)S(6)} %select_n.85), kind=kOutput, calls=%fused_computation.4.clone.1 | convolution fusion | flops 1082130432 | bytes 29360772 | tf_op jit(solution)/shard_map/while/body/eval_jaxpr/tab,tbf->taf/dot_general | solution.py:23
  76.2 0.8 compare_select_fusion.8
  76.9 38.1 %scatter_fusion = f32[32,128,256]{2,1,0:T(8,128)} fusion(f32[32,128,256]{2,1,0:T(8,128)} %get-tuple-element.409, s32[128]{0:T(128)S(1)} %compare_select_fusion.8, f32[128,128,256]{2,1,0:T(8,128)} %convolution_multiply_fusion.4), kind=kCustom, calls=%fused_computation.2.clone.1 | custom fusion | flops 4194304 | bytes 50332160 | tf_op jit(solution)/shard_map/while/body/eval_jaxpr/scatter-add | solution.py:27
  115.0 0.8 compare_and_fusion.4
  115.8 8.8 gather_fusion
  124.5 12.8 %convolution_multiply_fusion.4 = f32[128,128,256]{2,1,0:T(8,128)} fusion(f32[128]{0:T(128)S(1)} %get-tuple-element.384, bf16[128,128,256]{2,1,0:T(8,128)(2,1)} %gather_fusion, pred[128]{0:T(512)(128)(4,1)S(1)} %get-tuple-element.386, bf16[512,128,128]{2,1,0:T(8,128)(2,1)} %get-tuple-element.422, s32[]{:T(128)S(6)} %select_n.85), kind=kOutput, calls=%fused_computation.4.clone.1 | convolution fusion | flops 1082130432 | bytes 29360772 | tf_op jit(solution)/shard_map/while/body/eval_jaxpr/tab,tbf->taf/dot_general | solution.py:23
  137.3 0.8 compare_select_fusion.8
  138.1 38.1 %scatter_fusion = f32[32,128,256]{2,1,0:T(8,128)} fusion(f32[32,128,256]{2,1,0:T(8,128)} %get-tuple-element.409, s32[128]{0:T(128)S(1)} %compare_select_fusion.8, f32[128,128,256]{2,1,0:T(8,128)} %convolution_multiply_fusion.4), kind=kCustom, calls=%fused_computation.2.clone.1 | custom fusion | flops 4194304 | bytes 50332160 | tf_op jit(solution)/shard_map/while/body/eval_jaxpr/scatter-add | solution.py:27
  176.2 0.8 compare_and_fusion.4
  176.9 8.8 gather_fusion
  185.7 12.8 %convolution_multiply_fusion.4 = f32[128,128,256]{2,1,0:T(8,128)} fusion(f32[128]{0:T(128)S(1)} %get-tuple-element.384, bf16[128,128,256]{2,1,0:T(8,128)(2,1)} %gather_fusion, pred[128]{0:T(512)(128)(4,1)S(1)} %get-tuple-element.386, bf16[512,128,128]{2,1,0:T(8,128)(2,1)} %get-tuple-element.422, s32[]{:T(128)S(6)} %select_n.85), kind=kOutput, calls=%fused_computation.4.clone.1 | convolution fusion | flops 1082130432 | bytes 29360772 | tf_op jit(solution)/shard_map/while/body/eval_jaxpr/tab,tbf->taf/dot_general | solution.py:23
  198.5 0.8 compare_select_fusion.8
  199.3 37.7 %scatter_fusion = f32[32,128,256]{2,1,0:T(8,128)} fusion(f32[32,128,256]{2,1,0:T(8,128)} %get-tuple-element.409, s32[128]{0:T(128)S(1)} %compare_select_fusion.8, f32[128,128,256]{2,1,0:T(8,128)} %convolution_multiply_fusion.4), kind=kCustom, calls=%fused_computation.2.clone.1 | custom fusion | flops 4194304 | bytes 50332160 | tf_op jit(solution)/shard_map/while/body/eval_jaxpr/scatter-add | solution.py:27
  237.0 0.8 compare_and_fusion.4
  237.7 8.8 gather_fusion
  246.5 12.8 %convolution_multiply_fusion.4 = f32[128,128,256]{2,1,0:T(8,128)} fusion(f32[128]{0:T(128)S(1)} %get-tuple-element.384, bf16[128,128,256]{2,1,0:T(8,128)(2,1)} %gather_fusion, pred[128]{0:T(512)(128)(4,1)S(1)} %get-tuple-element.386, bf16[512,128,128]{2,1,0:T(8,128)(2,1)} %get-tuple-element.422, s32[]{:T(128)S(6)} %select_n.85), kind=kOutput, calls=%fused_computation.4.clone.1 | convolution fusion | flops 1082130432 | bytes 29360772 | tf_op jit(solution)/shard_map/while/body/eval_jaxpr/tab,tbf->taf/dot_general | solution.py:23
  259.3 0.8 compare_select_fusion.8
  260.1 37.9 %scatter_fusion = f32[32,128,256]{2,1,0:T(8,128)} fusion(f32[32,128,256]{2,1,0:T(8,128)} %get-tuple-element.409, s32[128]{0:T(128)S(1)} %compare_select_fusion.8, f32[128,128,256]{2,1,0:T(8,128)} %convolution_multiply_fusion.4), kind=kCustom, calls=%fused_computation.2.clone.1 | custom fusion | flops 4194304 | bytes 50332160 | tf_op jit(solution)/shard_map/while/body/eval_jaxpr/scatter-add | solution.py:27
  298.0 0.0 all-gather.5.cloned.1.call-start
  298.0 83.2 %reduce-scatter.3.cloned.1.call-done = f32[512,256]{1,0:T(8,128)} async-done(((f32[4096,256]{1,0:T(8,128)}), f32[512,256]{1,0:T(8,128)}) %reduce-scatter.3.cloned.1.call-update) | async-done | bytes 524304 | tf_op jit(solution)/shard_map/reduce_scatter | solution.py:51
  381.3 2.1 multiply_convert_fusion
  383.4 0.0 all-gather.5.cloned.1.call-update
  383.4 0.2 reduce-scatter.5.cloned.1.call-start
  383.6 22.4 %copy.10 = bf16[1,1,512,128,128]{3,4,2,1,0:T(8,128)(2,1)} copy(bf16[1,1,512,128,128]{4,3,2,1,0:T(8,128)(2,1)} %bitcast.21) | data formatting | bytes 33554432 | tf_op args[5]
  406.0 31.9 %all-gather.5.cloned.1.call-done = bf16[4096,256]{1,0:T(8,128)(2,1)} async-done(((bf16[512,256]{1,0:T(8,128)(2,1)}), bf16[4096,256]{1,0:T(8,128)(2,1)}) %all-gather.5.cloned.1.call-update) | async-done | bytes 2097168 | tf_op jit(solution)/shard_map/all_gather | solution.py:54
  437.9 4.2 broadcast_in_dim.75
  442.1 236.8 %while.27 = (s32[]{:T(128)}, f32[64,128,256]{2,1,0:T(8,128)}, s32[512]{0:T(512)}, bf16[512,128,128]{1,2,0:T(8,128)(2,1)}, s32[512]{0:T(512)}, /*index=5*/bf16[32...) while((s32[]{:T(128)}, f32[64,128,256]{2,1,0:T(8,128)}, ...), condition=%wide.region_6.7_spmd, body=%wide.region_4.6_spmd.sunk | while | flops 1086327040 | bytes 96478248 | solution.py:30
  442.1 0.8 compare_and_fusion.5
  442.9 6.6 gather_fusion.1
  449.5 12.8 %convolution_multiply_fusion.5 = f32[128,128,256]{2,1,0:T(8,128)} fusion(f32[128]{0:T(128)S(1)} %get-tuple-element.394, bf16[128,128,256]{2,1,0:T(8,128)(2,1)} %gather_fusion.1, pred[128]{0:T(512)(128)(4,1)S(1)} %get-tuple-element.396, bf16[512,128,128]{1,2,0:T(8,128)(2,1)} %get-tuple-element.455, s32[]{:T(128)S(6)} %select_n.88), kind=kOutput, calls=%fused_computation.16.clone.1 | convolution fusion | flops 1082130432 | bytes 29360772 | tf_op jit(solution)/shard_map/while/body/eval_jaxpr/tba,tbf->taf/dot_general | solution.py:23
  462.3 0.8 compare_select_fusion.9
  463.1 38.5 %scatter_fusion.1 = f32[64,128,256]{2,1,0:T(8,128)} fusion(f32[64,128,256]{2,1,0:T(8,128)} %get-tuple-element.442, s32[128]{0:T(128)S(1)} %compare_select_fusion.9, f32[128,128,256]{2,1,0:T(8,128)} %convolution_multiply_fusion.5), kind=kCustom, calls=%fused_computation.3.clone.1 | custom fusion | flops 4194304 | bytes 50332160 | tf_op jit(solution)/shard_map/while/body/eval_jaxpr/scatter-add | solution.py:27
  501.6 0.8 compare_and_fusion.5
  502.3 6.6 gather_fusion.1
  508.9 12.8 %convolution_multiply_fusion.5 = f32[128,128,256]{2,1,0:T(8,128)} fusion(f32[128]{0:T(128)S(1)} %get-tuple-element.394, bf16[128,128,256]{2,1,0:T(8,128)(2,1)} %gather_fusion.1, pred[128]{0:T(512)(128)(4,1)S(1)} %get-tuple-element.396, bf16[512,128,128]{1,2,0:T(8,128)(2,1)} %get-tuple-element.455, s32[]{:T(128)S(6)} %select_n.88), kind=kOutput, calls=%fused_computation.16.clone.1 | convolution fusion | flops 1082130432 | bytes 29360772 | tf_op jit(solution)/shard_map/while/body/eval_jaxpr/tba,tbf->taf/dot_general | solution.py:23
  521.7 0.8 compare_select_fusion.9
  522.5 38.1 %scatter_fusion.1 = f32[64,128,256]{2,1,0:T(8,128)} fusion(f32[64,128,256]{2,1,0:T(8,128)} %get-tuple-element.442, s32[128]{0:T(128)S(1)} %compare_select_fusion.9, f32[128,128,256]{2,1,0:T(8,128)} %convolution_multiply_fusion.5), kind=kCustom, calls=%fused_computation.3.clone.1 | custom fusion | flops 4194304 | bytes 50332160 | tf_op jit(solution)/shard_map/while/body/eval_jaxpr/scatter-add | solution.py:27
  560.6 0.8 compare_and_fusion.5
  561.3 6.6 gather_fusion.1
  567.9 12.8 %convolution_multiply_fusion.5 = f32[128,128,256]{2,1,0:T(8,128)} fusion(f32[128]{0:T(128)S(1)} %get-tuple-element.394, bf16[128,128,256]{2,1,0:T(8,128)(2,1)} %gather_fusion.1, pred[128]{0:T(512)(128)(4,1)S(1)} %get-tuple-element.396, bf16[512,128,128]{1,2,0:T(8,128)(2,1)} %get-tuple-element.455, s32[]{:T(128)S(6)} %select_n.88), kind=kOutput, calls=%fused_computation.16.clone.1 | convolution fusion | flops 1082130432 | bytes 29360772 | tf_op jit(solution)/shard_map/while/body/eval_jaxpr/tba,tbf->taf/dot_general | solution.py:23
  580.7 0.8 compare_select_fusion.9
  581.5 38.3 %scatter_fusion.1 = f32[64,128,256]{2,1,0:T(8,128)} fusion(f32[64,128,256]{2,1,0:T(8,128)} %get-tuple-element.442, s32[128]{0:T(128)S(1)} %compare_select_fusion.9, f32[128,128,256]{2,1,0:T(8,128)} %convolution_multiply_fusion.5), kind=kCustom, calls=%fused_computation.3.clone.1 | custom fusion | flops 4194304 | bytes 50332160 | tf_op jit(solution)/shard_map/while/body/eval_jaxpr/scatter-add | solution.py:27
  619.8 0.8 compare_and_fusion.5
  620.5 6.6 gather_fusion.1
  627.1 12.8 %convolution_multiply_fusion.5 = f32[128,128,256]{2,1,0:T(8,128)} fusion(f32[128]{0:T(128)S(1)} %get-tuple-element.394, bf16[128,128,256]{2,1,0:T(8,128)(2,1)} %gather_fusion.1, pred[128]{0:T(512)(128)(4,1)S(1)} %get-tuple-element.396, bf16[512,128,128]{1,2,0:T(8,128)(2,1)} %get-tuple-element.455, s32[]{:T(128)S(6)} %select_n.88), kind=kOutput, calls=%fused_computation.16.clone.1 | convolution fusion | flops 1082130432 | bytes 29360772 | tf_op jit(solution)/shard_map/while/body/eval_jaxpr/tba,tbf->taf/dot_general | solution.py:23
  639.9 0.8 compare_select_fusion.9
  640.7 38.3 %scatter_fusion.1 = f32[64,128,256]{2,1,0:T(8,128)} fusion(f32[64,128,256]{2,1,0:T(8,128)} %get-tuple-element.442, s32[128]{0:T(128)S(1)} %compare_select_fusion.9, f32[128,128,256]{2,1,0:T(8,128)} %convolution_multiply_fusion.5), kind=kCustom, calls=%fused_computation.3.clone.1 | custom fusion | flops 4194304 | bytes 50332160 | tf_op jit(solution)/shard_map/while/body/eval_jaxpr/scatter-add | solution.py:27
  679.0 0.0 all-reduce.3.cloned.1.call-start
  679.1 71.8 %reduce-scatter.5.cloned.1.call-done = f32[512,256]{1,0:T(8,128)} async-done(((f32[8192,256]{1,0:T(8,128)}), f32[512,256]{1,0:T(8,128)}) %reduce-scatter.5.cloned.1.call-update) | async-done | bytes 524304 | tf_op jit(solution)/shard_map/reduce_scatter | solution.py:65
  750.8 2.0 convolution_bitcast_fusion
  752.8 0.0 all-reduce.5.cloned.1.call-start
  752.9 119.6 %all-reduce.3.cloned.1.call-done = f32[256,256]{0,1:T(8,128)} async-done(((f32[256,256]{0,1:T(8,128)}), f32[256,256]{0,1:T(8,128)}) %all-reduce.3.cloned.1.call-update) | async-done | bytes 262160 | tf_op jit(solution)/shard_map/psum | solution.py:72
  872.6 2.0 convolution_convert_fusion
  874.6 80.4 %all-reduce.5.cloned.1.call-done = f32[256,256]{0,1:T(8,128)} async-done(((f32[256,256]{0,1:T(8,128)}), f32[256,256]{0,1:T(8,128)}) %all-reduce.5.cloned.1.call-update) | async-done | bytes 262160 | tf_op jit(solution)/shard_map/psum | solution.py:72
  954.9 1.8 copy.12
  (21 shorter events, 0.1 us)
Async XLA Ops:
  7.2 1.0 copy-start
  7.2 44.2 %all-gather.3.cloned.1.call-start = ((), (), s32[]{:S(2)}) async-start(), calls=%async_computation.2 | async-start | bytes 4456448 | tf_op jit(solution)/shard_map/all_gather | solution.py:47
  10.0 371.3 %reduce-scatter.3.cloned.1.call-start = ((), (), s32[]{:S(2)}) async-start(), calls=%async_computation.3 | async-start | bytes 4718592 | tf_op jit(solution)/shard_map/reduce_scatter | solution.py:51
  53.8 327.5 %copy-start.3 = (bf16[512,256]{1,0:T(8,128)(2,1)S(1)}, bf16[512,256]{1,0:T(8,128)(2,1)}, u32[]{:S(2)}) copy-start(bf16[512,256]{1,0:T(8,128)(2,1)} %param.13) | copy-start | bytes 786436
  298.0 139.9 %all-gather.5.cloned.1.call-start = ((), (), s32[]{:S(2)}) async-start(), calls=%async_computation.4 | async-start | bytes 2359296 | tf_op jit(solution)/shard_map/all_gather | solution.py:54
  383.4 367.4 %reduce-scatter.5.cloned.1.call-start = ((), (), s32[]{:S(2)}) async-start(), calls=%async_computation.5 | async-start | bytes 8912896 | tf_op jit(solution)/shard_map/reduce_scatter | solution.py:65
  437.9 4.2 copy-start.1
  679.0 193.6 %copy-start.2 = (bf16[256,256]{1,0:T(8,128)(2,1)S(1)}, bf16[256,256]{1,0:T(8,128)(2,1)}, u32[]{:S(2)}) copy-start(bf16[256,256]{1,0:T(8,128)(2,1)} %param.12) | copy-start | bytes 393220
  679.0 193.5 %all-reduce.3.cloned.1.call-start = ((), (), s32[]{:S(2)}) async-start(), calls=%async_computation.6 | async-start | bytes 524288 | tf_op jit(solution)/shard_map/psum | solution.py:72
  752.8 202.1 %all-reduce.5.cloned.1.call-start = ((), (), s32[]{:S(2)}) async-start(), calls=%async_computation.7 | async-start | bytes 524288 | tf_op jit(solution)/shard_map/psum | solution.py:72
Sparse Core Ops, SparseCore 0:
  10.3 41.0 all-gather.2
  298.1 83.1 reduce-scatter.2
  384.2 53.6 all-gather.4
  679.1 71.6 reduce-scatter.4
  753.7 118.7 all-reduce.2
  875.0 79.8 all-reduce.4
